TPU v7x, 256 devices: a whole 4x4x8 slice. The times are simulated.
256 devices in a mesh: lon: 64 (over z, x, y_hi), probe: 4 (over y_lo, core).
Axes of the slice: x: 4, y: 4 (y_hi: 2, y_lo: 2; y = y_hi * 2 + y_lo), z: 8, core: 2. Of those that a mesh axis runs over, the one named last changes fastest.
Arguments:
- increments: float32 [64, 1536, 8, 256], P('probe', 'lon'), may hold values from -6 to 6
- winds: float32 [2, 1536, 8, 256], P(None, 'lon'), may hold values from -0.2 to 0.2
- obs_weight: float32 [1536, 8, 256], P('lon'), may hold values from 0.1 to 10
Outputs:
- basis: float32 [64, 384, 512], P('probe', 'lon')
- upper: float32 [64, 64], replicated
All inputs are finite; a program needn't handle non-finite values.
Results may differ from a plain program's by a relative error of at most 0.00011.
Values sent between devices are 32-bit elements; how exact they have to be, the bound alone decides.
A program may use at most 128 MiB of HBM per device.

v0:
```python
import jax
import jax.numpy as jnp
from jax import lax
from jax.sharding import PartitionSpec as P


def from_behind(block, axis, distance):
    devices = range(lax.axis_size(axis))
    route = [((i - distance) % len(devices), i) for i in devices]
    return lax.ppermute(block, axis, route)


def padded(block, sides, width):
    for axis, dim in sides:
        count = lax.axis_size(axis)
        forward = [(i, i + 1) for i in range(count - 1)]
        forward.append((count - 1, 0))
        backward = [(target, source) for source, target in forward]
        low = lax.ppermute(
            lax.slice_in_dim(block, block.shape[dim] - width, None, axis=dim), axis, forward
        )
        high = lax.ppermute(lax.slice_in_dim(block, 0, width, axis=dim), axis, backward)
        block = jnp.concatenate([low, block, high], axis=dim)
    return block


def lat_mask(field):
    rows = lax.broadcasted_iota(jnp.int32, field.shape, field.ndim - 1)
    return jnp.where(rows > 0, field, jnp.zeros_like(field))


def below(field):
    return jnp.concatenate([jnp.zeros_like(field[..., :1]), field[..., :-1]], axis=-1)


def above(field):
    return jnp.concatenate([field[..., 1:], jnp.zeros_like(field[..., :1])], axis=-1)


def forward_core(widened, east, north):
    a_pos = jnp.maximum(east, 0.0)
    b_neg = jnp.minimum(east, 0.0)
    c_pos = jnp.maximum(north[1:-1], 0.0)
    d_neg = jnp.minimum(north[1:-1], 0.0)
    flux_w = a_pos[1:] * widened[:, :-1] + b_neg[1:] * widened[:, 1:]
    inner = widened[:, 1:-1]
    flux_s = c_pos * below(inner) + d_neg * inner
    flux_n = above(flux_s)
    return inner - (flux_w[:, 1:] - flux_w[:, :-1]) - (flux_n - flux_s)


def adjoint_core(widened, east, north):
    a_pos = jnp.maximum(east, 0.0)
    b_neg = jnp.minimum(east, 0.0)[1:-1]
    c_pos = jnp.maximum(north[1:-1], 0.0)
    d_neg = jnp.minimum(north[1:-1], 0.0)
    a_east = a_pos[2:]
    c_north = above(c_pos)
    inner = widened[:, 1:-1]
    west_val = widened[:, :-2]
    east_val = widened[:, 2:]
    return (
        inner * (1.0 - a_east + b_neg - c_north + d_neg)
        - b_neg * west_val
        + a_east * east_val
        - d_neg * below(inner)
        + c_north * above(inner)
    )


def body(increments, winds, obs_weight):
    east_local = winds[0]
    north_local = lat_mask(winds[1])
    next_first = from_behind(east_local[:1], "lon", -1)
    near_east = jnp.concatenate([jnp.zeros_like(next_first), east_local, next_first], axis=0)
    edge_zero = jnp.zeros_like(north_local[:1])
    near_north = jnp.concatenate([edge_zero, north_local, edge_zero], axis=0)

    def widen(field):
        return padded(field, (("lon", 1),), 1)

    state = increments
    for step in range(2):
        state = forward_core(widen(state), near_east, near_north)
    state = obs_weight * state
    for step in range(2):
        state = adjoint_core(widen(state), near_east, near_north)
    sketch = increments + state
    probe_count, lon_count, level_count, lat_count = sketch.shape
    coarse = jnp.mean(
        sketch.reshape(probe_count, lon_count // 4, 4, level_count, lat_count // 4, 4), axis=(2, 5)
    )
    coarse = coarse.reshape(probe_count, -1)
    all_probes = probe_count * lax.axis_size("probe")
    ident = jnp.eye(all_probes, dtype=jnp.float32)
    full_panel = lax.all_gather(coarse, "probe", axis=0, tiled=True)
    local_gram = jnp.dot(
        full_panel,
        full_panel.T,
        precision=lax.Precision.HIGHEST,
        preferred_element_type=jnp.float32,
    )
    gram = lax.psum(local_gram, "lon")
    lower = jnp.linalg.cholesky(gram)
    inverse = lax.linalg.triangular_solve(lower, ident, left_side=True, lower=True)
    own_rows = lax.dynamic_slice_in_dim(
        inverse, lax.axis_index("probe") * probe_count, probe_count, 0
    )
    basis = jnp.dot(
        own_rows, full_panel, precision=lax.Precision.HIGHEST, preferred_element_type=jnp.float32
    )
    return (basis.reshape(probe_count, lon_count // 4, -1), lower.T)


def solution(mesh):
    in_specs = (P("probe", "lon", None, None), P(None, "lon", None, None), P("lon", None, None))
    out_specs = (P("probe", "lon", None), P())
    return jax.shard_map(body, mesh=mesh, in_specs=in_specs, out_specs=out_specs, check_vma=False)
```

profile of v0, /device:TPU:8, one launch (start us, length us, event | category | flops | bytes accessed | tf_op | source)
XLA Modules:
  0.0 485.5 jit_solution(4162303472473665741)
XLA Ops:
  0.6 0.7 slice_bitcast_fusion.1
  1.3 9.8 %collective-permute-start = (f32[1,8,256]{2,1,0:T(8,128)S(1)}, f32[1,8,256]{2,1,0:T(8,128)S(1)}, u32[]{:S(2)}, u32[]{:S(2)}) collective-permute-start(f32[1,8,256]{2,1,0:T(8,128)S(1)} %slice_bitcast_fusion.1), channel_id=1, source_target_pairs={{4,0},{8,4},{12,8},{16,12},{20,16},{24,20},{28,24},{32,28},{36,32}... | collective-permute-start | bytes 24584 | tf_op jit(solution)/shard_map/ppermute | solution.py:10
  11.1 1.7 fusion.34
  12.8 0.0 collective-permute-start.1
  12.8 7.7 %collective-permute-start.2 = (f32[16,1,8,256]{3,2,1,0:T(8,128)}, f32[16,1,8,256]{3,2,1,0:T(8,128)}, u32[]{:S(2)}, u32[]{:S(2)}) collective-permute-start(f32[16,1,8,256]{3,2,1,0:T(8,128)} %get-tuple-element.22), channel_id=1, source_target_pairs={{4,0},{8,4},{12,8},{16,12},{20,16},{24,20},{28,24},{32,28},{36,32}... | collective-permute-start | bytes 393224 | tf_op jit(solution)/shard_map/ppermute | solution.py:22
  20.6 1.1 maximum_bitcast_fusion
  21.6 0.0 copy-start.4
  21.6 1.0 bitcast_select_fusion
  22.7 3.8 multiply_add_fusion.1
  26.5 0.0 copy-done.7
  26.5 0.0 copy-done.4
  26.5 0.0 copy-start.1
  26.5 0.9 slice_maximum_fusion
  27.4 0.8 copy-done.1
  28.2 2.6 slice.164
  30.7 0.5 pad.25.clone
  31.2 0.0 collective-permute-done
  31.3 0.7 fusion.21
  32.1 1.1 minimum_add_fusion
  33.2 0.0 collective-permute-done.1
  33.2 0.0 collective-permute-done.2
  33.2 0.0 copy-done
  33.2 1.5 fusion
  34.7 0.5 copy-done.2
  35.2 1.0 copy-done.3
  36.1 0.9 fusion.19
  37.1 0.1 collective-permute-start.3
  37.1 7.7 %collective-permute-start.4 = (f32[16,1,8,256]{3,2,1,0:T(8,128)S(1)}, f32[16,1,8,256]{3,2,1,0:T(8,128)S(1)}, u32[]{:S(2)}, u32[]{:S(2)}) collective-permute-start(f32[16,1,8,256]{3,2,1,0:T(8,128)S(1)} %get-tuple-element.20), channel_id=1, source_target_pairs={{4,0},{8,4},{12,8},{16,12},{20,16},{24,20},{28,24},{32,28},{36,32}... | collective-permute-start | bytes 393224 | tf_op jit(solution)/shard_map/ppermute | solution.py:22
  44.9 0.0 copy-done.5
  44.9 1.0 multiply_add_fusion
  45.9 2.5 slice.170
  48.4 0.0 collective-permute-done.3
  48.4 0.0 collective-permute-done.4
  48.4 0.4 fusion.1
  48.8 0.5 copy-done.6
  49.3 2.8 fusion.17
  52.2 0.1 collective-permute-start.5
  52.3 7.7 %collective-permute-start.6 = (f32[16,1,8,256]{3,2,1,0:T(8,128)S(1)}, f32[16,1,8,256]{3,2,1,0:T(8,128)S(1)}, u32[]{:S(2)}, u32[]{:S(2)}) collective-permute-start(f32[16,1,8,256]{3,2,1,0:T(8,128)S(1)} %get-tuple-element.19), channel_id=1, source_target_pairs={{4,0},{8,4},{12,8},{16,12},{20,16},{24,20},{28,24},{32,28},{36,32}... | collective-permute-start | bytes 393224 | tf_op jit(solution)/shard_map/ppermute | solution.py:22
  60.0 1.1 fusion.31
  61.1 1.8 collective-permute-done.5
  63.0 0.0 collective-permute-done.6
  63.0 2.2 fusion.12
  65.2 0.1 collective-permute-start.7
  65.3 7.8 %collective-permute-start.8 = (f32[16,1,8,256]{3,2,1,0:T(8,128)S(1)}, f32[16,1,8,256]{3,2,1,0:T(8,128)S(1)}, u32[]{:S(2)}, u32[]{:S(2)}) collective-permute-start(f32[16,1,8,256]{3,2,1,0:T(8,128)S(1)} %get-tuple-element.15), channel_id=1, source_target_pairs={{4,0},{8,4},{12,8},{16,12},{20,16},{24,20},{28,24},{32,28},{36,32}... | collective-permute-start | bytes 393224 | tf_op jit(solution)/shard_map/ppermute | solution.py:22
  73.1 1.2 fusion.29
  74.3 1.7 collective-permute-done.7
  76.0 0.0 collective-permute-done.8
  76.0 3.7 fusion.6
  79.6 13.4 %copy.25 = f32[16,24,8,256]{0,2,3,1:T(8,128)} copy(f32[16,24,8,256]{3,2,1,0:T(8,128)} %fusion.6) | data formatting | bytes 6291456 | tf_op jit(solution)/shard_map/add | solution.py:88
  93.0 10.1 %reduce_sum.9 = f32[16,6,8,64]{0,2,3,1:T(8,128)S(1)} reduce(f32[16,6,4,8,64,4]{0,3,5,4,2,1:T(8,128)} %bitcast.36, f32[]{:T(128)} %constant.53.clone.1), dimensions={2,5}, to_apply=%region_0.1 | reduce | flops 737280 | bytes 3342340 | tf_op jit(solution)/shard_map/reduce_sum | solution.py:90
  103.2 0.5 copy.26
  103.7 0.2 div.18
  103.9 8.5 %all_gather.3 = f32[64,3072]{1,0:T(8,128)S(1)} all-gather(f32[16,3072]{1,0:T(8,128)S(1)} %div.18), channel_id=1, replica_groups=mesh['lon'=64,'probe'=4] {'probe'}, dimensions={0}, use_global_device_ids=true | all-gather | bytes 983040 | tf_op jit(solution)/shard_map/all_gather | solution.py:96
  112.3 0.8 fusion.35
  113.1 358.1 %psum.7 = f32[64,64]{0,1:T(8,128)S(1)} all-reduce(f32[64,64]{0,1:T(8,128)S(1)} %fusion.35), channel_id=1, replica_groups=mesh['lon'=64,'probe'=4] {'lon'}, use_global_device_ids=true, to_apply=%region_1.2 | all-reduce | flops 4096 | bytes 32768 | tf_op jit(solution)/shard_map/psum | solution.py:103
  471.2 0.1 copy.28
  471.2 5.8 %cholesky.17 = f32[64,64]{1,0:T(8,128)S(1)} custom-call(f32[64,64]{1,0:T(8,128)S(1)} %fusion.24), custom_call_target="Cholesky" | custom-call | tf_op jit(solution)/shard_map/jit(cholesky)/cholesky | solution.py:104
  477.1 0.6 compare_reduce_fusion
  477.8 0.7 fusion.25
  478.4 4.9 %custom-call.6 = f32[1,64,64]{1,2,0:T(8,128)S(1)} custom-call(f32[1,64,64]{2,1,0:T(8,128)S(1)} %get-tuple-element.34), custom_call_target="InvertDiagBlocksLowerTriangular" | custom-call | tf_op jit(solution)/shard_map/triangular_solve | solution.py:105
  483.3 0.2 fusion.22
  483.6 0.5 fusion.26
  484.1 0.7 copy.34
  484.8 0.7 copy.30
  (15 shorter events, 0.2 us)
Async XLA Ops:
  1.3 29.9 %collective-permute-start = (f32[1,8,256]{2,1,0:T(8,128)S(1)}, f32[1,8,256]{2,1,0:T(8,128)S(1)}, u32[]{:S(2)}, u32[]{:S(2)}) collective-permute-start(f32[1,8,256]{2,1,0:T(8,128)S(1)} %slice_bitcast_fusion.1), channel_id=1, source_target_pairs={{4,0},{8,4},{12,8},{16,12},{20,16},{24,20},{28,24},{32,28},{36,32}... | collective-permute-start | bytes 24584 | tf_op jit(solution)/shard_map/ppermute | solution.py:10
  12.8 20.4 %collective-permute-start.1 = (f32[16,1,8,256]{3,2,1,0:T(8,128)}, f32[16,1,8,256]{3,2,1,0:T(8,128)}, u32[]{:S(2)}, u32[]{:S(2)}) collective-permute-start(f32[16,1,8,256]{3,2,1,0:T(8,128)} %get-tuple-element.23), channel_id=1, source_target_pairs={{0,4},{4,8},{8,12},{12,16},{16,20},{20,24},{24,28},{28,32},{32,36}... | collective-permute-start | bytes 393224 | tf_op jit(solution)/shard_map/ppermute | solution.py:19
  12.8 20.4 %collective-permute-start.2 = (f32[16,1,8,256]{3,2,1,0:T(8,128)}, f32[16,1,8,256]{3,2,1,0:T(8,128)}, u32[]{:S(2)}, u32[]{:S(2)}) collective-permute-start(f32[16,1,8,256]{3,2,1,0:T(8,128)} %get-tuple-element.22), channel_id=1, source_target_pairs={{4,0},{8,4},{12,8},{16,12},{20,16},{24,20},{28,24},{32,28},{36,32}... | collective-permute-start | bytes 393224 | tf_op jit(solution)/shard_map/ppermute | solution.py:22
  20.6 5.9 %copy-start.7 = (pred[256]{0:T(512)(128)(4,1)}, pred[256]{0:T(512)(128)(4,1)S(1)}, u32[]{:S(2)}) copy-start(pred[256]{0:T(512)(128)(4,1)S(1)} %iota_compare_fusion.3) | copy-start | bytes 772
  21.6 4.8 copy-start.4
  26.5 1.7 copy-start.1
  28.2 5.0 %copy-start = (f32[16,24,8,256]{3,2,1,0:T(8,128)S(1)}, f32[16,24,8,256]{3,2,1,0:T(8,128)}, u32[]{:S(2)}) copy-start(f32[16,24,8,256]{3,2,1,0:T(8,128)} %param.3) | copy-start | bytes 9437188
  33.2 2.0 copy-start.2
  33.2 3.0 copy-start.3
  36.1 8.8 %copy-start.5 = (f32[24,8,256]{2,1,0:T(8,128)S(1)}, f32[24,8,256]{2,1,0:T(8,128)}, u32[]{:S(2)}) copy-start(f32[24,8,256]{2,1,0:T(8,128)} %copy-done.4) | copy-start | bytes 589828
  37.1 11.3 %collective-permute-start.3 = (f32[16,1,8,256]{3,2,1,0:T(8,128)S(1)}, f32[16,1,8,256]{3,2,1,0:T(8,128)S(1)}, u32[]{:S(2)}, u32[]{:S(2)}) collective-permute-start(f32[16,1,8,256]{3,2,1,0:T(8,128)S(1)} %get-tuple-element.21), channel_id=1, source_target_pairs={{0,4},{4,8},{8,12},{12,16},{16,20},{20,24},{24,28},{28,32},{32,36}... | collective-permute-start | bytes 393224 | tf_op jit(solution)/shard_map/ppermute | solution.py:19
  37.1 11.2 %collective-permute-start.4 = (f32[16,1,8,256]{3,2,1,0:T(8,128)S(1)}, f32[16,1,8,256]{3,2,1,0:T(8,128)S(1)}, u32[]{:S(2)}, u32[]{:S(2)}) collective-permute-start(f32[16,1,8,256]{3,2,1,0:T(8,128)S(1)} %get-tuple-element.20), channel_id=1, source_target_pairs={{4,0},{8,4},{12,8},{16,12},{20,16},{24,20},{28,24},{32,28},{36,32}... | collective-permute-start | bytes 393224 | tf_op jit(solution)/shard_map/ppermute | solution.py:22
  48.4 0.9 copy-start.6
  52.2 10.8 %collective-permute-start.5 = (f32[16,1,8,256]{3,2,1,0:T(8,128)S(1)}, f32[16,1,8,256]{3,2,1,0:T(8,128)S(1)}, u32[]{:S(2)}, u32[]{:S(2)}) collective-permute-start(f32[16,1,8,256]{3,2,1,0:T(8,128)S(1)} %get-tuple-element.18), channel_id=1, source_target_pairs={{0,4},{4,8},{8,12},{12,16},{16,20},{20,24},{24,28},{28,32},{32,36}... | collective-permute-start | bytes 393224 | tf_op jit(solution)/shard_map/ppermute | solution.py:19
  52.3 10.7 %collective-permute-start.6 = (f32[16,1,8,256]{3,2,1,0:T(8,128)S(1)}, f32[16,1,8,256]{3,2,1,0:T(8,128)S(1)}, u32[]{:S(2)}, u32[]{:S(2)}) collective-permute-start(f32[16,1,8,256]{3,2,1,0:T(8,128)S(1)} %get-tuple-element.19), channel_id=1, source_target_pairs={{4,0},{8,4},{12,8},{16,12},{20,16},{24,20},{28,24},{32,28},{36,32}... | collective-permute-start | bytes 393224 | tf_op jit(solution)/shard_map/ppermute | solution.py:22
  65.2 10.8 %collective-permute-start.7 = (f32[16,1,8,256]{3,2,1,0:T(8,128)S(1)}, f32[16,1,8,256]{3,2,1,0:T(8,128)S(1)}, u32[]{:S(2)}, u32[]{:S(2)}) collective-permute-start(f32[16,1,8,256]{3,2,1,0:T(8,128)S(1)} %get-tuple-element.14), channel_id=1, source_target_pairs={{0,4},{4,8},{8,12},{12,16},{16,20},{20,24},{24,28},{28,32},{32,36}... | collective-permute-start | bytes 393224 | tf_op jit(solution)/shard_map/ppermute | solution.py:19
  65.3 10.7 %collective-permute-start.8 = (f32[16,1,8,256]{3,2,1,0:T(8,128)S(1)}, f32[16,1,8,256]{3,2,1,0:T(8,128)S(1)}, u32[]{:S(2)}, u32[]{:S(2)}) collective-permute-start(f32[16,1,8,256]{3,2,1,0:T(8,128)S(1)} %get-tuple-element.15), channel_id=1, source_target_pairs={{4,0},{8,4},{12,8},{16,12},{20,16},{24,20},{28,24},{32,28},{36,32}... | collective-permute-start | bytes 393224 | tf_op jit(solution)/shard_map/ppermute | solution.py:22
where the time goes:
time: 486 us; the launch traced here: 485 us
  blocking collectives  367 us (76%)
  other arithmetic  43.3 us (9%)
  starting transfers between devices  41.1 us (8%)
  local copies, waits for them, and re-layouts  28.6 us (6%)
    psum x1, blocking collectives, body(): gram = lax.psum(local_gram, 'lon')  358 us
    ppermute x4, starting transfers between devices, padded(): lax.ppermute(lax.slice_in_dim(block, 0, width, axis=dim), axis, backward)  31 us
    add x1, local copies, waits for them, and re-layouts, body(): sketch = increments + state  13.4 us
    reduce_sum x1, other arithmetic, body(): jnp.mean(sketch.reshape(probe_count, lon_count // 4, 4, level_count, lat_...  10.1 us
    ppermute x1, starting transfers between devices, from_behind(): return lax.ppermute(block, axis, route)  9.78 us
  transfers between devices with their start and end apart: 9, of which 2 were waited for; matrix products, arithmetic and copies ran while one was open for 4% of the time, Pallas kernels for 0%

commit v1 on v0

--- a/solution.py
+++ b/solution.py
@@ -100,7 +100,7 @@
         precision=lax.Precision.HIGHEST,
         preferred_element_type=jnp.float32,
     )
-    gram = lax.psum(local_gram, "lon")
+    gram = jax.lax.all_gather(local_gram, axis_name="lon").sum(axis=0)
     lower = jnp.linalg.cholesky(gram)
     inverse = lax.linalg.triangular_solve(lower, ident, left_side=True, lower=True)
     own_rows = lax.dynamic_slice_in_dim(

time: 486 us -> 251 us (0.52)
  blocking collectives: 367 us -> 8.45 us
  waiting for transfers between devices: 3.54 us -> 120 us
  between operations: 0.92 us -> 14.4 us
  local copies, waits for them, and re-layouts: 28.6 us -> 23.1 us
    psum x1 -> x0, blocking collectives: 358 us -> none  [body(): gram = lax.psum(local_gram, 'lon')]
    all_gather x0 -> x1, waiting for transfers between devices: none -> 116 us  [body(): gram = jax.lax.all_gather(local_gram, axis_name='lon').sum(axis=0)]
  transfers between devices with their start and end apart: 9 -> 10, of which waited for: 2 -> 3; matrix products, arithmetic and copies ran while one was open for 4% -> 5% of each run, Pallas kernels for 0% -> 0%
where the time goes in v1:
time: 251 us; the launch traced here: 250 us
  waiting for transfers between devices  120 us (48%)
  starting transfers between devices  41.2 us (16%)
  other arithmetic  40.5 us (16%)
  local copies, waits for them, and re-layouts  23.1 us (9%)
  between operations  14.4 us (6%)
  blocking collectives  8.45 us (3%)
    all_gather x1, waiting for transfers between devices, body(): gram = jax.lax.all_gather(local_gram, axis_name='lon').sum(axis=0)  116 us
    ppermute x4, starting transfers between devices, padded(): lax.ppermute(lax.slice_in_dim(block, 0, width, axis=dim), axis, backward)  31 us
    add x1, local copies, waits for them, and re-layouts, body(): sketch = increments + state  12.1 us
    reduce_sum x1, other arithmetic, body(): jnp.mean(sketch.reshape(probe_count, lon_count // 4, 4, level_count, lat_...  10.1 us
    ppermute x1, starting transfers between devices, from_behind(): return lax.ppermute(block, axis, route)  9.78 us
    all_gather x1, blocking collectives, body(): full_panel = lax.all_gather(coarse, 'probe', axis=0, tiled=True)  8.45 us
    another operation x3, other arithmetic, body(): lower = jnp.linalg.cholesky(gram)  6.52 us
  transfers between devices with their start and end apart: 10, of which 3 were waited for; matrix products, arithmetic and copies ran while one was open for 5% of the time, Pallas kernels for 0%

profile of v1, /device:TPU:8, one launch (start us, length us, event | category | flops | bytes accessed | tf_op | source)
XLA Modules:
  0.0 249.5 jit_solution(16360069103900305089)
XLA Ops:
  7.2 0.0 all-gather.3.cloned.1.call-start
  7.2 0.7 slice_bitcast_fusion.1
  7.9 9.8 %collective-permute-start = (f32[1,8,256]{2,1,0:T(8,128)S(1)}, f32[1,8,256]{2,1,0:T(8,128)S(1)}, u32[]{:S(2)}, u32[]{:S(2)}) collective-permute-start(f32[1,8,256]{2,1,0:T(8,128)S(1)} %slice_bitcast_fusion.1), channel_id=1, source_target_pairs={{4,0},{8,4},{12,8},{16,12},{20,16},{24,20},{28,24},{32,28},{36,32}... | collective-permute-start | bytes 24584 | tf_op jit(solution)/shard_map/ppermute | solution.py:10
  17.7 1.0 fusion.34
  18.7 0.1 collective-permute-start.1
  18.8 7.7 %collective-permute-start.2 = (f32[16,1,8,256]{3,2,1,0:T(8,128)S(1)}, f32[16,1,8,256]{3,2,1,0:T(8,128)S(1)}, u32[]{:S(2)}, u32[]{:S(2)}) collective-permute-start(f32[16,1,8,256]{3,2,1,0:T(8,128)S(1)} %get-tuple-element.22), channel_id=1, source_target_pairs={{4,0},{8,4},{12,8},{16,12},{20,16},{24,20},{28,24},{32,28},{36,32}... | collective-permute-start | bytes 393224 | tf_op jit(solution)/shard_map/ppermute | solution.py:22
  26.5 1.1 maximum_bitcast_fusion
  27.6 0.9 bitcast_select_fusion
  28.5 3.7 %multiply_add_fusion.1 = f32[16,24,8,256]{3,2,1,0:T(8,128)S(1)} fusion(f32[16,24,8,256]{3,2,1,0:T(8,128)} %param.3, f32[16,24,8,255]{3,2,1,0:T(8,128)} %bitcast.38, f32[24,8,256]{2,1,0:T(8,128)S(1)} %get-tuple-element.25, f32[24,8,256]{2,1,0:T(8,128)S(1)} %get-tuple-element.24), kind=kLoop, calls=%fused_computation.31 | loop fusion | flops 2359296 | bytes 9818112 | tf_op jit(solution)/shard_map/add | solution.py:47
  32.3 0.1 slice_maximum_fusion
  32.4 0.0 copy-start.7
  32.4 0.0 copy-start
  32.4 0.9 slice.164
  33.3 0.0 collective-permute-done
  33.3 0.1 fusion.21
  33.5 0.1 minimum_add_fusion
  33.6 0.0 copy-start.5
  33.6 0.0 collective-permute-done.1
  33.6 0.0 collective-permute-done.2
  33.6 0.8 copy-done
  34.4 0.4 fusion
  34.8 1.0 fusion.19
  35.8 0.1 collective-permute-start.3
  35.9 7.7 %collective-permute-start.4 = (f32[16,1,8,256]{3,2,1,0:T(8,128)S(1)}, f32[16,1,8,256]{3,2,1,0:T(8,128)S(1)}, u32[]{:S(2)}, u32[]{:S(2)}) collective-permute-start(f32[16,1,8,256]{3,2,1,0:T(8,128)S(1)} %get-tuple-element.20), channel_id=1, source_target_pairs={{4,0},{8,4},{12,8},{16,12},{20,16},{24,20},{28,24},{32,28},{36,32}... | collective-permute-start | bytes 393224 | tf_op jit(solution)/shard_map/ppermute | solution.py:22
  43.7 1.0 multiply_add_fusion
  44.6 2.5 %slice.170 = f32[16,24,8,255]{3,2,1,0:T(8,128)} slice(f32[16,24,8,256]{3,2,1,0:T(8,128)S(1)} %multiply_add_fusion), slice={[0:16], [0:24], [0:8], [1:256]} | slice | bytes 6266880 | tf_op jit(solution)/shard_map/slice | solution.py:37
  47.2 0.0 collective-permute-done.3
  47.2 0.0 collective-permute-done.4
  47.2 0.4 fusion.1
  47.6 0.5 copy-done.8
  48.1 2.8 %fusion.17 = f32[16,24,8,256]{3,2,1,0:T(8,128)S(1)} fusion(f32[16,24,8,256]{3,2,1,0:T(8,128)S(1)} %fusion.19, f32[16,25,8,256]{3,2,1,0:T(8,128)S(1)} %fusion.1, f32[16,24,8,256]{3,2,1,0:T(8,128)S(1)} %multiply_add_fusion, f32[16,24,8,255]{3,2,1,0:T(8,128)} %slice.170, f32[24,8,256]{2,1,0:T(8,128)S(1)} %copy-done.8), kind=kLoop, calls=%fused_computation.26 | loop fusion | flops 3932160 | bytes 19058688 | tf_op jit(solution)/shard_map/mul | solution.py:85
  51.0 0.1 collective-permute-start.5
  51.0 7.7 %collective-permute-start.6 = (f32[16,1,8,256]{3,2,1,0:T(8,128)S(1)}, f32[16,1,8,256]{3,2,1,0:T(8,128)S(1)}, u32[]{:S(2)}, u32[]{:S(2)}) collective-permute-start(f32[16,1,8,256]{3,2,1,0:T(8,128)S(1)} %get-tuple-element.19), channel_id=1, source_target_pairs={{4,0},{8,4},{12,8},{16,12},{20,16},{24,20},{28,24},{32,28},{36,32}... | collective-permute-start | bytes 393224 | tf_op jit(solution)/shard_map/ppermute | solution.py:22
  58.8 1.1 fusion.31
  59.9 1.8 collective-permute-done.5
  61.7 0.0 collective-permute-done.6
  61.7 0.0 copy-done.5
  61.7 2.2 fusion.12
  64.0 0.1 collective-permute-start.7
  64.1 0.0 copy-start.2
  64.1 0.0 copy-start.6
  64.1 7.8 %collective-permute-start.8 = (f32[16,1,8,256]{3,2,1,0:T(8,128)S(1)}, f32[16,1,8,256]{3,2,1,0:T(8,128)S(1)}, u32[]{:S(2)}, u32[]{:S(2)}) collective-permute-start(f32[16,1,8,256]{3,2,1,0:T(8,128)S(1)} %get-tuple-element.15), channel_id=1, source_target_pairs={{4,0},{8,4},{12,8},{16,12},{20,16},{24,20},{28,24},{32,28},{36,32}... | collective-permute-start | bytes 393224 | tf_op jit(solution)/shard_map/ppermute | solution.py:22
  71.9 1.2 fusion.29
  73.1 1.7 collective-permute-done.7
  74.8 0.0 collective-permute-done.8
  74.8 2.6 %fusion.6 = f32[16,24,8,256]{3,2,1,0:T(8,128)S(1)} fusion(f32[16,24,8,256]{3,2,1,0:T(8,128)S(1)} %copy-done, f32[16,1,8,256]{3,2,1,0:T(8,128)S(1)} %collective-permute-done.8, f32[16,24,8,256]{3,2,1,0:T(8,128)S(1)} %fusion.12, f32[16,1,8,256]{3,2,1,0:T(8,128)S(1)} %collective-permute-done.7, f32[16,24,8,255]{3,2,1,0:T(8,128)S(1)} %get-tuple-element.13, ...), kind=kLoop, calls=%fused_computation.11 | loop fusion | flops 9437184 | bytes 16949248 | tf_op jit(solution)/shard_map/add | solution.py:88
  77.4 12.1 %copy.21 = f32[16,24,8,256]{0,2,3,1:T(8,128)} copy(f32[16,24,8,256]{3,2,1,0:T(8,128)S(1)} %fusion.6) | data formatting | bytes 6291456 | tf_op jit(solution)/shard_map/add | solution.py:88
  89.5 10.1 %reduce_sum.18 = f32[16,6,8,64]{0,2,3,1:T(8,128)S(1)} reduce(f32[16,6,4,8,64,4]{0,3,5,4,2,1:T(8,128)} %bitcast.37, f32[]{:T(128)} %constant.53.clone.1), dimensions={2,5}, to_apply=%region_0.1 | reduce | flops 737280 | bytes 3342340 | tf_op jit(solution)/shard_map/reduce_sum | solution.py:90
  99.7 0.5 copy.22
  100.2 0.2 div.18
  100.4 8.5 %all_gather.9 = f32[64,3072]{1,0:T(8,128)S(1)} all-gather(f32[16,3072]{1,0:T(8,128)S(1)} %div.18), channel_id=1, replica_groups=mesh['lon'=64,'probe'=4] {'probe'}, dimensions={0}, use_global_device_ids=true | all-gather | bytes 983040 | tf_op jit(solution)/shard_map/all_gather | solution.py:96
  108.8 1.4 fusion.35
  110.2 0.0 all-gather.3.cloned.1.call-update
  110.3 116.3 %all-gather.3.cloned.1.call-done = f32[4096,64]{1,0:T(8,128)} async-done(((f32[64,64]{1,0:T(8,128)}), f32[4096,64]{1,0:T(8,128)}) %all-gather.3.cloned.1.call-update) | async-done | bytes 1048592 | tf_op jit(solution)/shard_map/all_gather | solution.py:103
  226.6 1.8 reduce_sum.19
  228.4 0.1 copy.23
  228.4 5.8 %cholesky.17 = f32[64,64]{1,0:T(8,128)S(1)} custom-call(f32[64,64]{1,0:T(8,128)S(1)} %fusion.24), custom_call_target="Cholesky" | custom-call | tf_op jit(solution)/shard_map/jit(cholesky)/cholesky | solution.py:104
  234.3 0.6 compare_reduce_fusion
  235.0 0.7 fusion.25
  235.6 4.9 %custom-call.6 = f32[1,64,64]{1,2,0:T(8,128)S(1)} custom-call(f32[1,64,64]{2,1,0:T(8,128)S(1)} %get-tuple-element.34), custom_call_target="InvertDiagBlocksLowerTriangular" | custom-call | tf_op jit(solution)/shard_map/triangular_solve | solution.py:105
  240.5 0.2 fusion.22
  240.8 0.5 fusion.26
  241.3 0.7 copy.28
  242.0 0.7 copy.25
  (20 shorter events, 0.2 us)
Async XLA Ops:
  7.2 219.4 %all-gather.3.cloned.1.call-start = ((), (), s32[]{:S(2)}) async-start(), calls=%async_computation | async-start | bytes 2129920 | tf_op jit(solution)/shard_map/all_gather | solution.py:103
  7.9 25.4 %collective-permute-start = (f32[1,8,256]{2,1,0:T(8,128)S(1)}, f32[1,8,256]{2,1,0:T(8,128)S(1)}, u32[]{:S(2)}, u32[]{:S(2)}) collective-permute-start(f32[1,8,256]{2,1,0:T(8,128)S(1)} %slice_bitcast_fusion.1), channel_id=1, source_target_pairs={{4,0},{8,4},{12,8},{16,12},{20,16},{24,20},{28,24},{32,28},{36,32}... | collective-permute-start | bytes 24584 | tf_op jit(solution)/shard_map/ppermute | solution.py:10
  18.7 14.9 %collective-permute-start.1 = (f32[16,1,8,256]{3,2,1,0:T(8,128)S(1)}, f32[16,1,8,256]{3,2,1,0:T(8,128)S(1)}, u32[]{:S(2)}, u32[]{:S(2)}) collective-permute-start(f32[16,1,8,256]{3,2,1,0:T(8,128)S(1)} %get-tuple-element.23), channel_id=1, source_target_pairs={{0,4},{4,8},{8,12},{12,16},{16,20},{20,24},{24,28},{28,32},{32,36}... | collective-permute-start | bytes 393224 | tf_op jit(solution)/shard_map/ppermute | solution.py:19
  18.8 14.8 %collective-permute-start.2 = (f32[16,1,8,256]{3,2,1,0:T(8,128)S(1)}, f32[16,1,8,256]{3,2,1,0:T(8,128)S(1)}, u32[]{:S(2)}, u32[]{:S(2)}) collective-permute-start(f32[16,1,8,256]{3,2,1,0:T(8,128)S(1)} %get-tuple-element.22), channel_id=1, source_target_pairs={{4,0},{8,4},{12,8},{16,12},{20,16},{24,20},{28,24},{32,28},{36,32}... | collective-permute-start | bytes 393224 | tf_op jit(solution)/shard_map/ppermute | solution.py:22
  32.4 1.1 copy-start.7
  32.4 2.0 copy-start
  33.5 28.2 %copy-start.1 = (f32[24,8,256]{2,1,0:T(8,128)}, f32[24,8,256]{2,1,0:T(8,128)S(1)}, u32[]{:S(2)}) copy-start(f32[24,8,256]{2,1,0:T(8,128)S(1)} %get-tuple-element.28) | copy-start | bytes 589828
  33.5 28.2 %copy-start.3 = (f32[24,8,256]{2,1,0:T(8,128)}, f32[24,8,256]{2,1,0:T(8,128)S(1)}, u32[]{:S(2)}) copy-start(f32[24,8,256]{2,1,0:T(8,128)S(1)} %get-tuple-element.29) | copy-start | bytes 589828
  33.6 28.2 %copy-start.5 = (f32[24,8,256]{2,1,0:T(8,128)}, f32[24,8,256]{2,1,0:T(8,128)S(1)}, u32[]{:S(2)}) copy-start(f32[24,8,256]{2,1,0:T(8,128)S(1)} %get-tuple-element.32) | copy-start | bytes 589828
  35.8 11.3 %collective-permute-start.3 = (f32[16,1,8,256]{3,2,1,0:T(8,128)S(1)}, f32[16,1,8,256]{3,2,1,0:T(8,128)S(1)}, u32[]{:S(2)}, u32[]{:S(2)}) collective-permute-start(f32[16,1,8,256]{3,2,1,0:T(8,128)S(1)} %get-tuple-element.21), channel_id=1, source_target_pairs={{0,4},{4,8},{8,12},{12,16},{16,20},{20,24},{24,28},{28,32},{32,36}... | collective-permute-start | bytes 393224 | tf_op jit(solution)/shard_map/ppermute | solution.py:19
  35.9 11.2 %collective-permute-start.4 = (f32[16,1,8,256]{3,2,1,0:T(8,128)S(1)}, f32[16,1,8,256]{3,2,1,0:T(8,128)S(1)}, u32[]{:S(2)}, u32[]{:S(2)}) collective-permute-start(f32[16,1,8,256]{3,2,1,0:T(8,128)S(1)} %get-tuple-element.20), channel_id=1, source_target_pairs={{4,0},{8,4},{12,8},{16,12},{20,16},{24,20},{28,24},{32,28},{36,32}... | collective-permute-start | bytes 393224 | tf_op jit(solution)/shard_map/ppermute | solution.py:22
  47.2 0.9 copy-start.8
  51.0 10.8 %collective-permute-start.5 = (f32[16,1,8,256]{3,2,1,0:T(8,128)S(1)}, f32[16,1,8,256]{3,2,1,0:T(8,128)S(1)}, u32[]{:S(2)}, u32[]{:S(2)}) collective-permute-start(f32[16,1,8,256]{3,2,1,0:T(8,128)S(1)} %get-tuple-element.18), channel_id=1, source_target_pairs={{0,4},{4,8},{8,12},{12,16},{16,20},{20,24},{24,28},{28,32},{32,36}... | collective-permute-start | bytes 393224 | tf_op jit(solution)/shard_map/ppermute | solution.py:19
  51.0 10.7 %collective-permute-start.6 = (f32[16,1,8,256]{3,2,1,0:T(8,128)S(1)}, f32[16,1,8,256]{3,2,1,0:T(8,128)S(1)}, u32[]{:S(2)}, u32[]{:S(2)}) collective-permute-start(f32[16,1,8,256]{3,2,1,0:T(8,128)S(1)} %get-tuple-element.19), channel_id=1, source_target_pairs={{4,0},{8,4},{12,8},{16,12},{20,16},{24,20},{28,24},{32,28},{36,32}... | collective-permute-start | bytes 393224 | tf_op jit(solution)/shard_map/ppermute | solution.py:22
  64.0 10.8 %collective-permute-start.7 = (f32[16,1,8,256]{3,2,1,0:T(8,128)S(1)}, f32[16,1,8,256]{3,2,1,0:T(8,128)S(1)}, u32[]{:S(2)}, u32[]{:S(2)}) collective-permute-start(f32[16,1,8,256]{3,2,1,0:T(8,128)S(1)} %get-tuple-element.14), channel_id=1, source_target_pairs={{0,4},{4,8},{8,12},{12,16},{16,20},{20,24},{24,28},{28,32},{32,36}... | collective-permute-start | bytes 393224 | tf_op jit(solution)/shard_map/ppermute | solution.py:19
  64.1 10.7 %copy-start.2 = (f32[24,8,256]{2,1,0:T(8,128)S(1)}, f32[24,8,256]{2,1,0:T(8,128)}, u32[]{:S(2)}) copy-start(f32[24,8,256]{2,1,0:T(8,128)} %copy-done.1) | copy-start | bytes 589828
  64.1 10.7 %copy-start.4 = (f32[24,8,256]{2,1,0:T(8,128)S(1)}, f32[24,8,256]{2,1,0:T(8,128)}, u32[]{:S(2)}) copy-start(f32[24,8,256]{2,1,0:T(8,128)} %copy-done.3) | copy-start | bytes 589828
  64.1 10.7 %copy-start.6 = (f32[24,8,256]{2,1,0:T(8,128)S(1)}, f32[24,8,256]{2,1,0:T(8,128)}, u32[]{:S(2)}) copy-start(f32[24,8,256]{2,1,0:T(8,128)} %copy-done.5) | copy-start | bytes 589828
  64.1 10.6 %collective-permute-start.8 = (f32[16,1,8,256]{3,2,1,0:T(8,128)S(1)}, f32[16,1,8,256]{3,2,1,0:T(8,128)S(1)}, u32[]{:S(2)}, u32[]{:S(2)}) collective-permute-start(f32[16,1,8,256]{3,2,1,0:T(8,128)S(1)} %get-tuple-element.15), channel_id=1, source_target_pairs={{4,0},{8,4},{12,8},{16,12},{20,16},{24,20},{28,24},{32,28},{36,32}... | collective-permute-start | bytes 393224 | tf_op jit(solution)/shard_map/ppermute | solution.py:22
Sparse Core Ops, SparseCore 0:
  110.4 116.1 all-gather.2
